TPU v7x, 32 devices: a whole 2x2x4 slice. The times are simulated.
32 devices in a mesh: seq: 2 (over x), ep: 16 (over z, y, core).
Axes of the slice: x: 2, y: 2, z: 4, core: 2. Of those that a mesh axis runs over, the one named last changes fastest.
Arguments:
- tokens: bfloat16 [256, 7168], P(('seq', 'ep')), may hold values from -50 to 50
- out_grad: bfloat16 [256, 7168], P(('seq', 'ep')), may hold values from -6 to 6
- routes: int32 [256, 8], P(('seq', 'ep')), may hold values from 0 to 15, all different within a row; in each aligned block of 8 rows (0 to 7, 8 to 15, ...) at most 5 rows name the same one
- gate_fixed: int32 [256, 8], P(('seq', 'ep')), may hold values from 1 to 65535
- ramp_step: int32 [16], replicated, may hold values from 1 to 8
- norm_gain: float32 [7168], replicated, may hold values from 0.1 to 1.9
- w_gate: bfloat16 [16, 7168, 1024], P('ep', None, 'seq'), may hold values from -0.0625 to 0.0625
- w_up: bfloat16 [16, 7168, 1024], P('ep', None, 'seq'), may hold values from -0.0625 to 0.0625
- w_down: bfloat16 [16, 1024, 7168], P('ep', 'seq'), may hold values from -0.1875 to 0.1875
Outputs:
- mixed: bfloat16 [256, 7168], P(('seq', 'ep'))
- tokens_grad: bfloat16 [256, 7168], P(('seq', 'ep'))
- gain_grad: float32 [7168], P(('seq', 'ep'))
- w_gate_grad: bfloat16 [16, 7168, 1024], P('ep', None, 'seq')
- w_up_grad: bfloat16 [16, 7168, 1024], P('ep', None, 'seq')
- w_down_grad: bfloat16 [16, 1024, 7168], P('ep', 'seq')
Inputs may be any that keep to these rules, and one draw needn't show every extreme that they name: `routes`: each row names 8 different experts. Within the rows of one device (aligned blocks of 8 rows) no expert is named more than 5 times, and in some such block one expert is named exactly 5 times.
All inputs are finite; a program needn't handle non-finite values.
Results may differ from a plain program's by a relative error of at most 0.023.
Values may be sent and summed in bfloat16 or wider, within the bound.
No kernel may reach another device: no remote copies, remote signals or barrier semaphores. Data moves between devices by JAX's collectives and lax.ppermute only.
A program may use at most 128 MiB of HBM per device.

v0:
```python
import jax
import jax.numpy as jnp
from jax import lax
from jax.sharding import PartitionSpec as P

RAMP = 8
gate_unit = 65536.0
norm_eps = 1e-06


def contract_rows(left, right):
    return lax.dot_general(
        left, right, (((0,), (0,)), ((), ())), preferred_element_type=jnp.float32
    )


def contract_cols(left, right):
    return lax.dot_general(
        left, right, (((1,), (1,)), ((), ())), preferred_element_type=jnp.float32
    )


def dispatch(send_normed, send_grad, seq_count, experts, capacity):
    width = send_normed.shape[1]

    def spread(buffer):
        wide = jnp.broadcast_to(
            buffer.reshape(1, experts, capacity, width), (seq_count, experts, capacity, width)
        )
        return wide.reshape(seq_count * experts, capacity, width)

    got_normed, got_grad = (
        lax.all_to_all(spread(send_normed), ("seq", "ep"), split_axis=0, concat_axis=0, tiled=True),
        lax.all_to_all(spread(send_grad), ("seq", "ep"), split_axis=0, concat_axis=0, tiled=True),
    )
    return (got_normed.reshape(-1, width), got_grad.reshape(-1, width))


def collect(out_part, back_part, seq_count, ep_count, capacity):
    width = out_part.shape[1]
    sum_out, sum_back = (
        lax.psum_scatter(
            out_part.reshape(seq_count, ep_count * capacity, width).astype(jnp.bfloat16),
            "seq",
            scatter_dimension=0,
            tiled=True,
        ).astype(jnp.float32),
        lax.psum_scatter(
            back_part.reshape(seq_count, ep_count * capacity, width).astype(jnp.bfloat16),
            "seq",
            scatter_dimension=0,
            tiled=True,
        ).astype(jnp.float32),
    )
    got_out, got_back = (
        lax.all_to_all(
            sum_out.astype(jnp.bfloat16).reshape(ep_count, capacity, width),
            "ep",
            split_axis=0,
            concat_axis=0,
            tiled=True,
        ),
        lax.all_to_all(
            sum_back.astype(jnp.bfloat16).reshape(ep_count, capacity, width),
            "ep",
            split_axis=0,
            concat_axis=0,
            tiled=True,
        ),
    )
    return (got_out.reshape(-1, width), got_back.reshape(-1, width))


def on_device(tokens, out_grad, routes, gate_fixed, ramp_step, norm_gain, w_gate, w_up, w_down):
    seq_count = lax.axis_size("seq")
    ep_count = lax.axis_size("ep")
    rows_dev, width = tokens.shape
    top_count = routes.shape[1]
    capacity = min(rows_dev, 5 * rows_dev * top_count // (4 * ep_count))
    tokens_wide = tokens.astype(jnp.float32)
    recip = lax.rsqrt(jnp.mean(tokens_wide * tokens_wide, axis=1, keepdims=True) + norm_eps)
    normed = (tokens_wide * recip * norm_gain[None, :]).astype(jnp.bfloat16)
    flat_routes = routes.reshape(-1)
    onehot = (flat_routes[:, None] == jnp.arange(ep_count, dtype=jnp.int32)[None, :]).astype(
        jnp.int32
    )
    position = jnp.sum(jnp.cumsum(onehot, axis=0) * onehot, axis=1) - 1
    slot_index = flat_routes * capacity + position
    ramp_pick = jnp.sum(onehot * ramp_step[None, :], axis=1).astype(jnp.float32)
    coef = gate_fixed.reshape(-1).astype(jnp.float32) / gate_unit * ramp_pick / RAMP
    grad_rows = (
        coef[:, None] * jnp.repeat(out_grad.astype(jnp.float32), top_count, axis=0)
    ).astype(jnp.bfloat16)
    normed_rows = jnp.repeat(normed, top_count, axis=0)
    empty = jnp.zeros((ep_count * capacity, width), jnp.bfloat16)
    send_normed = empty.at[slot_index].set(normed_rows)
    send_grad = empty.at[slot_index].set(grad_rows)
    in_normed, in_grad = dispatch(send_normed, send_grad, seq_count, ep_count, capacity)
    weight_gate = w_gate[0]
    weight_up = w_up[0]
    weight_down = w_down[0]
    pre_gate = jnp.dot(in_normed, weight_gate, preferred_element_type=jnp.float32)
    pre_up = jnp.dot(in_normed, weight_up, preferred_element_type=jnp.float32)
    sigma = jax.nn.sigmoid(pre_gate)
    active = pre_gate * sigma
    hidden = (active * pre_up).astype(jnp.bfloat16)
    out_part = jnp.dot(hidden, weight_down, preferred_element_type=jnp.float32)
    hidden_grad = contract_cols(in_grad, weight_down)
    gate_pre_grad = (hidden_grad * pre_up * sigma * (1.0 + pre_gate * (1.0 - sigma))).astype(
        jnp.bfloat16
    )
    up_pre_grad = (hidden_grad * active).astype(jnp.bfloat16)
    w_down_grad = contract_rows(hidden, in_grad).astype(jnp.bfloat16)[None]
    w_gate_grad = contract_rows(in_normed, gate_pre_grad).astype(jnp.bfloat16)[None]
    w_up_grad = contract_rows(in_normed, up_pre_grad).astype(jnp.bfloat16)[None]
    back_part = contract_cols(gate_pre_grad, weight_gate) + contract_cols(up_pre_grad, weight_up)
    slot_out, slot_back = collect(out_part, back_part, seq_count, ep_count, capacity)
    picked_out = slot_out[slot_index].astype(jnp.float32).reshape(rows_dev, top_count, width)
    picked_back = slot_back[slot_index].astype(jnp.float32).reshape(rows_dev, top_count, width)
    mixed = jnp.sum(coef.reshape(rows_dev, top_count, 1) * picked_out, axis=1).astype(jnp.bfloat16)
    normed_grad = jnp.sum(picked_back, axis=1)
    gain_term = jnp.sum(normed_grad * tokens_wide * recip, axis=0)
    gain_grad = lax.psum_scatter(gain_term, ("seq", "ep"), scatter_dimension=0, tiled=True)
    scaled = norm_gain[None, :] * normed_grad
    inner = jnp.sum(scaled * tokens_wide, axis=1, keepdims=True)
    tokens_grad = (recip * scaled - tokens_wide * recip * recip * recip * inner / width).astype(
        jnp.bfloat16
    )
    return (mixed, tokens_grad, gain_grad, w_gate_grad, w_up_grad, w_down_grad)


def solution(mesh):
    return jax.shard_map(
        on_device,
        mesh=mesh,
        in_specs=(
            P(("seq", "ep"), None),
            P(("seq", "ep"), None),
            P(("seq", "ep"), None),
            P(("seq", "ep"), None),
            P(),
            P(),
            P("ep", None, "seq"),
            P("ep", None, "seq"),
            P("ep", "seq", None),
        ),
        out_specs=(
            P(("seq", "ep"), None),
            P(("seq", "ep"), None),
            P(("seq", "ep")),
            P("ep", None, "seq"),
            P("ep", None, "seq"),
            P("ep", "seq", None),
        ),
        check_vma=False,
    )
```

profile of v0, /device:TPU:0, one launch (start us, length us, event | category | flops | bytes accessed | tf_op | source)
XLA Modules:
  0.0 395.7 jit_solution(4662358553127045000)
XLA Ops:
  7.2 0.8 eq.15
  7.9 0.7 broadcast_multiply_fusion
  8.6 1.1 fusion.34
  9.7 0.1 mul.148
  9.8 0.1 fusion.38
  9.9 0.1 reduce_window_sum.11
  10.0 0.8 select_reduce_fusion.1
  10.8 1.0 fusion.28
  11.8 2.2 scatter_custom_fusion
  14.0 0.6 broadcast_in_dim.22
  14.6 2.3 broadcast_in_dim.46
  16.8 0.0 copy-start.3
  16.8 0.0 copy-start.2
  16.8 7.4 %all-to-all-start = ((bf16[32,5,7168]{2,1,0:T(8,128)(2,1)}), bf16[32,5,7168]{2,1,0:T(8,128)(2,1)}, u32[]{:S(2)}, u32[]{:S(2)}) async-start(bf16[32,5,7168]{2,1,0:T(8,128)(2,1)} %bitcast.62), calls=%async_computation | async-start | bytes 7340032 | tf_op jit(solution)/shard_map/all_to_all | solution.py:33
  24.3 0.1 convert_element_type.90
  24.3 0.0 copy-done.3
  24.4 0.1 div.36
  24.4 0.0 copy-done.2
  24.5 2.2 scatter_custom_fusion.1
  26.7 0.6 broadcast_in_dim.48
  27.3 80.6 %all-to-all-done = bf16[32,5,7168]{2,1,0:T(8,128)(2,1)} async-done(((bf16[32,5,7168]{2,1,0:T(8,128)(2,1)}), bf16[32,5,7168]{2,1,0:T(8,128)(2,1)}, u32[]{:S(2)}, u32[]{:S(2)}) %all-to-all-start) | async-done | bytes 2293792 | tf_op jit(solution)/shard_map/all_to_all | solution.py:33
  107.8 2.2 broadcast_in_dim.49
  110.1 3.5 all-to-all-start.2
  113.6 0.0 reduce-scatter.3.cloned.1.call-start
  113.7 3.3 reshape.132
  117.0 4.4 %fusion.8 = f32[160,512]{1,0:T(8,128)S(1)} fusion(bf16[160,7168]{1,0:T(8,128)(2,1)S(1)} %reshape.132, bf16[1,7168,512]{2,1,0:T(8,128)(2,1)} %param.16), kind=kOutput, calls=%fused_computation.17 | convolution fusion | flops 1174405120 | bytes 9961472 | tf_op jit(solution)/shard_map/dot_general | solution.py:103
  121.4 4.4 %fusion.12 = f32[160,512]{1,0:T(8,128)S(1)} fusion(bf16[160,7168]{1,0:T(8,128)(2,1)S(1)} %reshape.132, bf16[1,7168,512]{2,1,0:T(8,128)(2,1)} %param.15), kind=kOutput, calls=%fused_computation.21 | convolution fusion | flops 1174405120 | bytes 9961472 | tf_op jit(solution)/shard_map/dot_general | solution.py:102
  125.8 71.4 %all-to-all-done.2 = bf16[32,5,7168]{2,1,0:T(8,128)(2,1)} async-done(((bf16[32,5,7168]{2,1,0:T(8,128)(2,1)}), bf16[32,5,7168]{2,1,0:T(8,128)(2,1)}, u32[]{:S(2)}, u32[]{:S(2)}) %all-to-all-start.2) | async-done | bytes 2293792 | tf_op jit(solution)/shard_map/all_to_all | solution.py:34
  197.3 4.6 %reshape.137 = bf16[160,7168]{1,0:T(8,128)(2,1)} reshape(bf16[32,5,7168]{2,1,0:T(8,128)(2,1)} %all-to-all-done.2) | data formatting | bytes 4587520 | tf_op jit(solution)/shard_map/reshape | solution.py:36
  201.8 6.4 %multiply_convert_fusion = (bf16[160,512]{1,0:T(8,128)(2,1)S(1)}, bf16[160,512]{1,0:T(8,128)(2,1)S(1)}, bf16[160,512]{1,0:T(8,128)(2,1)S(1)}) fusion(f32[160,512]{1,0:T(8,128)S(1)} %fusion.12, f32[160,512]{1,0:T(8,128)S(1)} %fusion.8, bf16[160,7168]{1,0:T(8,128)(2,1)} %reshape.137, bf16[1,512,7168]{2,1,0:T(8,128)(2,1)} %param.17), kind=kOutput, calls=%fused_computation.40 | convolution fusion | flops 1175633920 | bytes 10780672 | tf_op jit(solution)/shard_map/dot_general | solution.py:18
  208.3 5.8 %convolution_convert_fusion.3 = bf16[2,80,7168]{2,1,0:T(8,128)(2,1)} fusion(bf16[2,80,512]{2,1,0:T(8,128)(2,1)S(1)} %bitcast.65, bf16[1,512,7168]{2,1,0:T(8,128)(2,1)} %param.17), kind=kOutput, calls=%fused_computation.12 | convolution fusion | flops 1175552000 | bytes 9797632 | tf_op jit(solution)/shard_map/dot_general | solution.py:107
  214.1 0.0 reduce-scatter.3.cloned.1.call-update
  214.1 0.2 reduce-scatter.5.cloned.1.call-start
  214.4 5.8 %fusion.10 = f32[160,7168]{1,0:T(8,128)S(1)} fusion(bf16[160,512]{1,0:T(8,128)(2,1)S(1)} %get-tuple-element.11, bf16[1,7168,512]{2,1,0:T(8,128)(2,1)} %param.15), kind=kOutput, calls=%fused_computation.19 | convolution fusion | flops 1174405120 | bytes 12091392 | tf_op jit(solution)/shard_map/dot_general | solution.py:18
  220.2 7.1 %fusion.3 = bf16[160,7168]{1,0:T(8,128)(2,1)} fusion(f32[160,7168]{1,0:T(8,128)S(1)} %fusion.10, bf16[160,512]{1,0:T(8,128)(2,1)S(1)} %get-tuple-element.10, bf16[1,7168,512]{2,1,0:T(8,128)(2,1)} %param.16), kind=kOutput, calls=%fused_computation.11 | convolution fusion | flops 1176698880 | bytes 14385152 | tf_op jit(solution)/shard_map/dot_general | solution.py:18
  227.2 0.0 reduce-scatter.5.cloned.1.call-update
  227.3 18.1 %reduce-scatter.3.cloned.1.call-done = bf16[1,80,7168]{2,1,0:T(8,128)(2,1)} async-done(((bf16[2,80,7168]{2,1,0:T(8,128)(2,1)}), bf16[1,80,7168]{2,1,0:T(8,128)(2,1)}) %reduce-scatter.3.cloned.1.call-update) | async-done | bytes 1146896 | tf_op jit(solution)/shard_map/reduce_scatter | solution.py:42
  245.4 2.5 reshape.133
  247.9 5.7 %all-to-all-start.1 = ((bf16[16,5,7168]{2,1,0:T(8,128)(2,1)}), bf16[16,5,7168]{2,1,0:T(8,128)(2,1)}, u32[]{:S(2)}, u32[]{:S(2)}) async-start(bf16[16,5,7168]{2,1,0:T(8,128)(2,1)} %reshape.133), calls=%async_computation.2 | async-start | bytes 3670016 | tf_op jit(solution)/shard_map/all_to_all | solution.py:56
  253.6 28.7 %reduce-scatter.5.cloned.1.call-done = bf16[1,80,7168]{2,1,0:T(8,128)(2,1)} async-done(((bf16[2,80,7168]{2,1,0:T(8,128)(2,1)}), bf16[1,80,7168]{2,1,0:T(8,128)(2,1)}) %reduce-scatter.5.cloned.1.call-update) | async-done | bytes 1146896 | tf_op jit(solution)/shard_map/reduce_scatter | solution.py:48
  282.3 2.5 reshape.138
  284.8 5.2 %all-to-all-done.1 = bf16[16,5,7168]{2,1,0:T(8,128)(2,1)} async-done(((bf16[16,5,7168]{2,1,0:T(8,128)(2,1)}), bf16[16,5,7168]{2,1,0:T(8,128)(2,1)}, u32[]{:S(2)}, u32[]{:S(2)}) %all-to-all-start.1) | async-done | bytes 1146912 | tf_op jit(solution)/shard_map/all_to_all | solution.py:56
  290.1 10.2 %all-to-all-start.3 = ((bf16[16,5,7168]{2,1,0:T(8,128)(2,1)}), bf16[16,5,7168]{2,1,0:T(8,128)(2,1)}, u32[]{:S(2)}, u32[]{:S(2)}) async-start(bf16[16,5,7168]{2,1,0:T(8,128)(2,1)} %reshape.138), calls=%async_computation.5 | async-start | bytes 3670016 | tf_op jit(solution)/shard_map/all_to_all | solution.py:63
  300.3 6.8 %fusion.2 = bf16[1,512,7168]{2,1,0:T(8,128)(2,1)} fusion(bf16[160,512]{1,0:T(8,128)(2,1)S(1)} %get-tuple-element.12, bf16[160,7168]{1,0:T(8,128)(2,1)} %reshape.137), kind=kOutput, calls=%fused_computation.9 | convolution fusion | flops 1178075136 | bytes 9797632 | tf_op jit(solution)/shard_map/dot_general | solution.py:12
  307.1 5.2 %fusion.1 = bf16[1,7168,512]{2,1,0:T(8,128)(2,1)} fusion(bf16[160,7168]{1,0:T(8,128)(2,1)S(1)} %reshape.132, bf16[160,512]{1,0:T(8,128)(2,1)S(1)} %get-tuple-element.10), kind=kOutput, calls=%fused_computation.8 | convolution fusion | flops 1178075136 | bytes 9797632 | tf_op jit(solution)/shard_map/dot_general | solution.py:12
  312.3 5.2 %fusion = bf16[1,7168,512]{2,1,0:T(8,128)(2,1)} fusion(bf16[160,7168]{1,0:T(8,128)(2,1)S(1)} %reshape.132, bf16[160,512]{1,0:T(8,128)(2,1)S(1)} %get-tuple-element.11), kind=kOutput, calls=%fused_computation.7 | convolution fusion | flops 1178075136 | bytes 9797632 | tf_op jit(solution)/shard_map/dot_general | solution.py:12
  317.4 1.7 reshape.134
  319.2 1.1 gather_fusion
  320.3 16.4 %all-to-all-done.3 = bf16[16,5,7168]{2,1,0:T(8,128)(2,1)} async-done(((bf16[16,5,7168]{2,1,0:T(8,128)(2,1)}), bf16[16,5,7168]{2,1,0:T(8,128)(2,1)}, u32[]{:S(2)}, u32[]{:S(2)}) %all-to-all-start.3) | async-done | bytes 1146912 | tf_op jit(solution)/shard_map/all_to_all | solution.py:63
  336.7 1.7 reshape.139
  338.5 0.0 copy-start
  338.5 0.0 copy-start.1
  338.5 1.1 gather_fusion.1
  339.6 0.6 convert_reduce_fusion
  340.2 0.0 copy-done
  340.3 0.0 copy-done.1
  340.3 0.2 fusion.37
  340.5 0.8 fusion.33
  341.3 45.5 %all-reduce = f32[7168]{0:T(1024)S(1)} all-reduce(f32[7168]{0:T(1024)S(1)} %get-tuple-element.6), channel_id=4, replica_groups=mesh['seq'=2,'ep'=16] {'seq','ep'}, use_global_device_ids=true, to_apply=%region_12.13.clone | all-reduce | flops 7168 | bytes 57344
  386.8 1.4 fusion.14
  388.2 0.6 dynamic-slice
  (7 shorter events, 0.1 us)
Async XLA Ops:
  16.8 7.5 %copy-start.3 = (s32[8,8]{1,0:T(8,128)S(1)}, s32[8,8]{1,0:T(8,128)}, u32[]{:S(2)}) copy-start(s32[8,8]{1,0:T(8,128)} %param.12) | copy-start | bytes 772
  16.8 7.6 %copy-start.2 = (bf16[8,7168]{1,0:T(8,128)(2,1)S(1)}, bf16[8,7168]{1,0:T(8,128)(2,1)}, u32[]{:S(2)}) copy-start(bf16[8,7168]{1,0:T(8,128)(2,1)} %param.10) | copy-start | bytes 344068
  16.8 91.0 %all-to-all-start = ((bf16[32,5,7168]{2,1,0:T(8,128)(2,1)}), bf16[32,5,7168]{2,1,0:T(8,128)(2,1)}, u32[]{:S(2)}, u32[]{:S(2)}) async-start(bf16[32,5,7168]{2,1,0:T(8,128)(2,1)} %bitcast.62), calls=%async_computation | async-start | bytes 7340032 | tf_op jit(solution)/shard_map/all_to_all | solution.py:33
  110.1 87.2 %all-to-all-start.2 = ((bf16[32,5,7168]{2,1,0:T(8,128)(2,1)}), bf16[32,5,7168]{2,1,0:T(8,128)(2,1)}, u32[]{:S(2)}, u32[]{:S(2)}) async-start(bf16[32,5,7168]{2,1,0:T(8,128)(2,1)} %bitcast.63), calls=%async_computation.3 | async-start | bytes 7340032 | tf_op jit(solution)/shard_map/all_to_all | solution.py:34
  113.6 131.7 %reduce-scatter.3.cloned.1.call-start = ((), (), s32[]{:S(2)}) async-start(), calls=%async_computation.6 | async-start | bytes 3440640 | tf_op jit(solution)/shard_map/reduce_scatter | solution.py:42
  214.1 68.2 %reduce-scatter.5.cloned.1.call-start = ((), (), s32[]{:S(2)}) async-start(), calls=%async_computation.7 | async-start | bytes 3440640 | tf_op jit(solution)/shard_map/reduce_scatter | solution.py:48
  247.9 42.1 %all-to-all-start.1 = ((bf16[16,5,7168]{2,1,0:T(8,128)(2,1)}), bf16[16,5,7168]{2,1,0:T(8,128)(2,1)}, u32[]{:S(2)}, u32[]{:S(2)}) async-start(bf16[16,5,7168]{2,1,0:T(8,128)(2,1)} %reshape.133), calls=%async_computation.2 | async-start | bytes 3670016 | tf_op jit(solution)/shard_map/all_to_all | solution.py:56
  290.1 46.7 %all-to-all-start.3 = ((bf16[16,5,7168]{2,1,0:T(8,128)(2,1)}), bf16[16,5,7168]{2,1,0:T(8,128)(2,1)}, u32[]{:S(2)}, u32[]{:S(2)}) async-start(bf16[16,5,7168]{2,1,0:T(8,128)(2,1)} %reshape.138), calls=%async_computation.5 | async-start | bytes 3670016 | tf_op jit(solution)/shard_map/all_to_all | solution.py:63
  338.5 1.8 copy-start
  338.5 1.8 copy-start.1
Sparse Core Ops, SparseCore 0:
  214.3 31.0 reduce-scatter.2
  248.2 34.0 reduce-scatter.4
where the time goes:
time: 397 us; the launch traced here: 396 us
  waiting for transfers between devices  220 us (55%)
  matrix products  51.1 us (13%)
  blocking collectives  45.5 us (11%)
  local copies, waits for them, and re-layouts  28.1 us (7%)
  starting transfers between devices  27.1 us (7%)
  between operations  14.3 us (4%)
  other arithmetic  9.08 us (2%)
    all_to_all x1, waiting for transfers between devices, dispatch(): lax.all_to_all(spread(send_normed), ('seq', 'ep'), split_axis=0, concat_a...  80.6 us
    all_to_all x1, waiting for transfers between devices, dispatch(): lax.all_to_all(spread(send_grad), ('seq', 'ep'), split_axis=0, concat_axi...  71.4 us
    unnamed x1, blocking collectives  45.5 us
    reduce_scatter x1, waiting for transfers between devices, collect(): lax.psum_scatter(back_part.reshape(seq_count, ep_count * capacity, width)...  28.7 us
    dot_general x3, matrix products, contract_cols(): lax.dot_general(left, right, (((1,), (1,)), ((), ())), preferred_element_...  19.3 us
    reduce_scatter x1, waiting for transfers between devices, collect(): lax.psum_scatter(out_part.reshape(seq_count, ep_count * capacity, width)....  18.1 us
    dot_general x3, matrix products, contract_rows(): lax.dot_general(left, right, (((0,), (0,)), ((), ())), preferred_element_...  17.1 us
    all_to_all x1, waiting for transfers between devices, collect(): lax.all_to_all(sum_back.astype(jnp.bfloat16).reshape(ep_count, capacity,...  16.4 us
  transfers between devices with their start and end apart: 6, of which 6 were waited for; matrix products, arithmetic and copies ran while one was open for 13% of the time, Pallas kernels for 0%

commit v1 on v0

--- a/solution.py
+++ b/solution.py
@@ -6,6 +6,30 @@
 RAMP = 8
 gate_unit = 65536.0
 norm_eps = 1e-06
+
+
+def in_blocks(array, dim, peers):
+    lengths = array.shape
+    blocks = array.reshape(*lengths[:dim], peers, lengths[dim] // peers, *lengths[dim + 1 :])
+    return jnp.moveaxis(blocks, dim, 0)
+
+
+def joined_along(blocks, dim):
+    shape = list(blocks.shape[1:])
+    shape[dim] *= blocks.shape[0]
+    return jnp.moveaxis(blocks, 0, dim).reshape(shape)
+
+
+def rotated_exchange(array, axis, split_dim, concat_dim):
+    size, index = (lax.axis_size(axis), lax.axis_index(axis))
+    blocks = in_blocks(array, split_dim, size)
+    result = blocks
+    for step in range(1, size):
+        target, source = ((index + step) % size, (index - step) % size)
+        sent = lax.dynamic_index_in_dim(blocks, target, 0)
+        received = lax.ppermute(sent, axis, [(i, (i + step) % size) for i in range(size)])
+        result = lax.dynamic_update_slice_in_dim(result, received, source, axis=0)
+    return joined_along(result, concat_dim)
 
 
 def contract_rows(left, right):
@@ -60,12 +84,8 @@
             concat_axis=0,
             tiled=True,
         ),
-        lax.all_to_all(
-            sum_back.astype(jnp.bfloat16).reshape(ep_count, capacity, width),
-            "ep",
-            split_axis=0,
-            concat_axis=0,
-            tiled=True,
+        rotated_exchange(
+            sum_back.astype(jnp.bfloat16).reshape(ep_count, capacity, width), "ep", 0, 0
         ),
     )
     return (got_out.reshape(-1, width), got_back.reshape(-1, width))

time: 397 us -> 458 us (1.15)
  waiting for transfers between devices: 220 us -> 259 us
  starting transfers between devices: 27.1 us -> 42.2 us
  local copies, waits for them, and re-layouts: 28.1 us -> 40.9 us
    ppermute x0 -> x15, waiting for transfers between devices: none -> 70.6 us  [rotated_exchange(): lax.ppermute(sent, axis, [(i, (i + step) % size) for i in range(size)])]
    ppermute x0 -> x15, starting transfers between devices: none -> 25.1 us  [rotated_exchange(): lax.ppermute(sent, axis, [(i, (i + step) % size) for i in range(size)])]
    all_to_all x1 -> x0, waiting for transfers between devices: 16.4 us -> none  [collect(): lax.all_to_all(sum_back.astype(jnp.bfloat16).reshape(ep_count, capacity,...]
    reduce_scatter x1, waiting for transfers between devices: 28.7 us -> 17.8 us  [collect(): lax.psum_scatter(back_part.reshape(seq_count, ep_count * capacity, width)...]
    all_to_all x1 -> x0, starting transfers between devices: 10.2 us -> none  [collect(): lax.all_to_all(sum_back.astype(jnp.bfloat16).reshape(ep_count, capacity,...]
    dynamic_update_slice x0 -> x14, local copies, waits for them, and re-layouts: none -> 9.17 us  [rotated_exchange(): result = lax.dynamic_update_slice_in_dim(result, received, source, axis=0)]
    all_to_all x1, waiting for transfers between devices: 5.21 us -> 0.01 us  [collect(): lax.all_to_all(sum_out.astype(jnp.bfloat16).reshape(ep_count, capacity, w...]
  transfers between devices with their start and end apart: 6 -> 20, of which waited for: 6 -> 14; matrix products, arithmetic and copies ran while one was open for 13% -> 13% of each run, Pallas kernels for 0% -> 0%
where the time goes in v1:
time: 458 us; the launch traced here: 457 us
  waiting for transfers between devices  259 us (57%)
  matrix products  48.4 us (11%)
  blocking collectives  43 us (9%)
  starting transfers between devices  42.2 us (9%)
  local copies, waits for them, and re-layouts  40.9 us (9%)
  between operations  15 us (3%)
  other arithmetic  9.08 us (2%)
    all_to_all x1, waiting for transfers between devices, dispatch(): lax.all_to_all(spread(send_normed), ('seq', 'ep'), split_axis=0, concat_a...  80.6 us
    all_to_all x1, waiting for transfers between devices, dispatch(): lax.all_to_all(spread(send_grad), ('seq', 'ep'), split_axis=0, concat_axi...  71.2 us
    ppermute x15, waiting for transfers between devices, rotated_exchange(): lax.ppermute(sent, axis, [(i, (i + step) % size) for i in range(size)])  70.6 us
    unnamed x1, blocking collectives  43 us
    ppermute x15, starting transfers between devices, rotated_exchange(): lax.ppermute(sent, axis, [(i, (i + step) % size) for i in range(size)])  25.1 us
    reduce_scatter x1, waiting for transfers between devices, collect(): lax.psum_scatter(out_part.reshape(seq_count, ep_count * capacity, width)....  18.3 us
    reduce_scatter x1, waiting for transfers between devices, collect(): lax.psum_scatter(back_part.reshape(seq_count, ep_count * capacity, width)...  17.8 us
    dot_general x3, matrix products, contract_rows(): lax.dot_general(left, right, (((0,), (0,)), ((), ())), preferred_element_...  17.2 us
  transfers between devices with their start and end apart: 20, of which 14 were waited for; matrix products, arithmetic and copies ran while one was open for 13% of the time, Pallas kernels for 0%

profile of v1, /device:TPU:0, one launch (start us, length us, event | category | flops | bytes accessed | tf_op | source)
XLA Modules:
  0.0 457.1 jit_solution(10134265108688122662)
XLA Ops:
  7.2 0.8 eq.46
  7.9 0.7 broadcast_multiply_fusion
  8.6 1.1 fusion.34
  10.0 0.8 select_reduce_fusion.1
  10.8 1.0 fusion.28
  11.8 2.2 scatter_custom_fusion
  14.6 2.4 broadcast_in_dim.46
  16.9 7.4 %all-to-all-start = ((bf16[32,5,7168]{2,1,0:T(8,128)(2,1)}), bf16[32,5,7168]{2,1,0:T(8,128)(2,1)}, u32[]{:S(2)}, u32[]{:S(2)}) async-start(bf16[32,5,7168]{2,1,0:T(8,128)(2,1)} %bitcast.66), calls=%async_computation | async-start | bytes 7340032 | tf_op jit(solution)/shard_map/all_to_all | solution.py:57
  24.6 2.2 scatter_custom_fusion.1
  27.4 80.6 %all-to-all-done = bf16[32,5,7168]{2,1,0:T(8,128)(2,1)} async-done(((bf16[32,5,7168]{2,1,0:T(8,128)(2,1)}), bf16[32,5,7168]{2,1,0:T(8,128)(2,1)}, u32[]{:S(2)}, u32[]{:S(2)}) %all-to-all-start) | async-done | bytes 2293792 | tf_op jit(solution)/shard_map/all_to_all | solution.py:57
  108.0 2.4 broadcast_in_dim.49
  110.4 3.5 all-to-all-start.2
  114.1 3.3 reshape.126
  117.4 4.4 fusion.8
  121.8 4.4 fusion.12
  126.3 71.2 %all-to-all-done.2 = bf16[32,5,7168]{2,1,0:T(8,128)(2,1)} async-done(((bf16[32,5,7168]{2,1,0:T(8,128)(2,1)}), bf16[32,5,7168]{2,1,0:T(8,128)(2,1)}, u32[]{:S(2)}, u32[]{:S(2)}) %all-to-all-start.2) | async-done | bytes 2293792 | tf_op jit(solution)/shard_map/all_to_all | solution.py:58
  197.5 4.6 %reshape.131 = bf16[160,7168]{1,0:T(8,128)(2,1)} reshape(bf16[32,5,7168]{2,1,0:T(8,128)(2,1)} %all-to-all-done.2) | data formatting | bytes 4587520 | tf_op jit(solution)/shard_map/reshape | solution.py:60
  202.1 6.6 %multiply_convert_fusion = (bf16[160,512]{1,0:T(8,128)(2,1)S(1)}, bf16[160,512]{1,0:T(8,128)(2,1)S(1)}, bf16[160,512]{1,0:T(8,128)(2,1)S(1)}) fusion(f32[160,512]{1,0:T(8,128)S(1)} %fusion.12, f32[160,512]{1,0:T(8,128)S(1)} %fusion.8, bf16[160,7168]{1,0:T(8,128)(2,1)} %reshape.131, bf16[1,512,7168]{2,1,0:T(8,128)(2,1)} %param.17), kind=kOutput, calls=%fused_computation.40 | convolution fusion | flops 1175633920 | bytes 10780672 | tf_op jit(solution)/shard_map/dot_general | solution.py:42
  208.7 5.8 %fusion.10 = f32[160,7168]{1,0:T(8,128)S(1)} fusion(bf16[160,512]{1,0:T(8,128)(2,1)S(1)} %get-tuple-element.26, bf16[1,7168,512]{2,1,0:T(8,128)(2,1)} %param.15), kind=kOutput, calls=%fused_computation.19 | convolution fusion | flops 1174405120 | bytes 12091392 | tf_op jit(solution)/shard_map/dot_general | solution.py:42
  214.5 4.0 fusion.3
  218.6 5.9 %convolution_convert_fusion.3 = bf16[2,80,7168]{2,1,0:T(8,128)(2,1)} fusion(bf16[2,80,512]{2,1,0:T(8,128)(2,1)S(1)} %bitcast.69, bf16[1,512,7168]{2,1,0:T(8,128)(2,1)} %param.17), kind=kOutput, calls=%fused_computation.12 | convolution fusion | flops 1175552000 | bytes 9797632 | tf_op jit(solution)/shard_map/dot_general | solution.py:127
  225.1 6.8 %fusion.2 = bf16[1,512,7168]{2,1,0:T(8,128)(2,1)} fusion(bf16[160,512]{1,0:T(8,128)(2,1)S(1)} %get-tuple-element.27, bf16[160,7168]{1,0:T(8,128)(2,1)} %reshape.131), kind=kOutput, calls=%fused_computation.9 | convolution fusion | flops 1178075136 | bytes 9797632 | tf_op jit(solution)/shard_map/dot_general | solution.py:36
  231.9 17.8 %reduce-scatter.5.cloned.1.call-done = bf16[1,80,7168]{2,1,0:T(8,128)(2,1)} async-done(((bf16[2,80,7168]{2,1,0:T(8,128)(2,1)}), bf16[1,80,7168]{2,1,0:T(8,128)(2,1)}) %reduce-scatter.5.cloned.1.call-update) | async-done | bytes 1146896 | tf_op jit(solution)/shard_map/reduce_scatter | solution.py:72
  249.8 2.6 reshape_reshape.6
  252.4 0.9 constant_dynamic-slice_fusion.14
  253.3 5.3 %fusion.1 = bf16[1,7168,512]{2,1,0:T(8,128)(2,1)} fusion(bf16[160,7168]{1,0:T(8,128)(2,1)S(1)} %reshape.126, bf16[160,512]{1,0:T(8,128)(2,1)S(1)} %get-tuple-element.25), kind=kOutput, calls=%fused_computation.8 | convolution fusion | flops 1178075136 | bytes 9797632 | tf_op jit(solution)/shard_map/dot_general | solution.py:36
  258.6 1.6 collective-permute-done
  260.2 2.4 constant_dynamic-slice_fusion
  262.7 5.2 %fusion = bf16[1,7168,512]{2,1,0:T(8,128)(2,1)} fusion(bf16[160,7168]{1,0:T(8,128)(2,1)S(1)} %reshape.126, bf16[160,512]{1,0:T(8,128)(2,1)S(1)} %get-tuple-element.26), kind=kOutput, calls=%fused_computation.7 | convolution fusion | flops 1178075136 | bytes 9797632 | tf_op jit(solution)/shard_map/dot_general | solution.py:36
  267.8 18.3 %reduce-scatter.3.cloned.1.call-done = bf16[1,80,7168]{2,1,0:T(8,128)(2,1)} async-done(((bf16[2,80,7168]{2,1,0:T(8,128)(2,1)}), bf16[1,80,7168]{2,1,0:T(8,128)(2,1)}) %reduce-scatter.3.cloned.1.call-update) | async-done | bytes 1146896 | tf_op jit(solution)/shard_map/reduce_scatter | solution.py:66
  286.1 2.6 reshape.127
  288.8 5.8 %all-to-all-start.1 = ((bf16[16,5,7168]{2,1,0:T(8,128)(2,1)}), bf16[16,5,7168]{2,1,0:T(8,128)(2,1)}, u32[]{:S(2)}, u32[]{:S(2)}) async-start(bf16[16,5,7168]{2,1,0:T(8,128)(2,1)} %reshape.127), calls=%async_computation.2 | async-start | bytes 3670016 | tf_op jit(solution)/shard_map/all_to_all | solution.py:80
  294.6 4.3 collective-permute-start.14
  300.1 1.4 collective-permute-start.2
  302.1 36.2 %collective-permute-done.2 = bf16[1,1,5,7168]{3,2,0,1:T(8,128)(2,1)S(1)} collective-permute-done((bf16[1,1,5,7168]{3,2,0,1:T(8,128)(2,1)S(1)}, bf16[1,1,5,7168]{3,2,0,1:T(8,128)(2,1)S(1)}, u32[]{:S(2)}, u32[]{:S(2)}) %collective-permute-start.2) | collective-permute-done | bytes 71712 | tf_op jit(solution)/shard_map/ppermute | solution.py:30
  339.0 6.0 %collective-permute-done.3 = bf16[1,1,5,7168]{3,2,0,1:T(8,128)(2,1)S(1)} collective-permute-done((bf16[1,1,5,7168]{3,2,0,1:T(8,128)(2,1)S(1)}, bf16[1,1,5,7168]{3,2,0,1:T(8,128)(2,1)S(1)}, u32[]{:S(2)}, u32[]{:S(2)}) %collective-permute-start.3) | collective-permute-done | bytes 71712 | tf_op jit(solution)/shard_map/ppermute | solution.py:30
  345.0 5.1 %collective-permute-start.4 = (bf16[1,1,5,7168]{3,2,0,1:T(8,128)(2,1)S(1)}, bf16[1,1,5,7168]{3,2,0,1:T(8,128)(2,1)S(1)}, u32[]{:S(2)}, u32[]{:S(2)}) collective-permute-start(bf16[1,1,5,7168]{3,2,0,1:T(8,128)(2,1)S(1)} %copy-done.6), channel_id=1, source_target_pairs={{0,5},{1,6},{2,7},{3,8},{4,9},{5,10},{6,11},{7,12},{8,13},{9,14},{... | collective-permute-start | bytes 215048 | tf_op jit(solution)/shard_map/ppermute | solution.py:30
  350.1 0.7 constant_dynamic-update-slice_fusion.10
  350.8 1.7 collective-permute-done.4
  352.5 1.1 collective-permute-start.5
  354.2 6.5 %collective-permute-done.5 = bf16[1,1,5,7168]{3,2,0,1:T(8,128)(2,1)S(1)} collective-permute-done((bf16[1,1,5,7168]{3,2,0,1:T(8,128)(2,1)S(1)}, bf16[1,1,5,7168]{3,2,0,1:T(8,128)(2,1)S(1)}, u32[]{:S(2)}, u32[]{:S(2)}) %collective-permute-start.5) | collective-permute-done | bytes 71712 | tf_op jit(solution)/shard_map/ppermute | solution.py:30
  360.7 0.7 constant_dynamic-update-slice_fusion.8
  361.3 4.5 collective-permute-done.6
  365.8 5.4 %collective-permute-start.7 = (bf16[1,1,5,7168]{3,2,0,1:T(8,128)(2,1)S(1)}, bf16[1,1,5,7168]{3,2,0,1:T(8,128)(2,1)S(1)}, u32[]{:S(2)}, u32[]{:S(2)}) collective-permute-start(bf16[1,1,5,7168]{3,2,0,1:T(8,128)(2,1)S(1)} %copy-done.3), channel_id=1, source_target_pairs={{0,8},{1,9},{2,10},{3,11},{4,12},{5,13},{6,14},{7,15},{8,0},{9,1},... | collective-permute-start | bytes 215048 | tf_op jit(solution)/shard_map/ppermute | solution.py:30
  371.2 0.7 constant_dynamic-update-slice_fusion.7
  371.9 5.3 %collective-permute-done.7 = bf16[1,1,5,7168]{3,2,0,1:T(8,128)(2,1)S(1)} collective-permute-done((bf16[1,1,5,7168]{3,2,0,1:T(8,128)(2,1)S(1)}, bf16[1,1,5,7168]{3,2,0,1:T(8,128)(2,1)S(1)}, u32[]{:S(2)}, u32[]{:S(2)}) %collective-permute-start.7) | collective-permute-done | bytes 71712 | tf_op jit(solution)/shard_map/ppermute | solution.py:30
  377.1 0.7 constant_dynamic-update-slice_fusion.6
  377.8 4.5 collective-permute-done.8
  382.3 2.8 collective-permute-start.9
  385.1 0.7 constant_dynamic-update-slice_fusion.5
  385.7 2.6 collective-permute-done.9
  388.4 3.7 collective-permute-start.10
  392.1 0.7 constant_dynamic-update-slice_fusion.4
  392.8 1.7 collective-permute-done.10
  394.5 0.7 constant_dynamic-update-slice_fusion.3
  395.8 0.7 constant_dynamic-update-slice_fusion.1
  396.5 0.7 constant_dynamic-update-slice_fusion
  397.8 1.7 reshape_reshape.7
  399.5 1.1 gather_fusion.1
  401.5 43.0 %all-reduce = f32[7168]{0:T(1024)S(1)} all-reduce(f32[7168]{0:T(1024)S(1)} %get-tuple-element.6), channel_id=4, replica_groups=mesh['seq'=2,'ep'=16] {'seq','ep'}, use_global_device_ids=true, to_apply=%region_12.13.clone | all-reduce | flops 7168 | bytes 57344
  445.2 0.8 fusion.33
  446.0 1.7 reshape.128
  447.7 1.1 gather_fusion
  448.8 1.4 fusion.14
  (65 shorter events, 8.0 us)
Async XLA Ops:
  16.9 7.5 %copy-start.9 = (s32[8,8]{1,0:T(8,128)S(1)}, s32[8,8]{1,0:T(8,128)}, u32[]{:S(2)}) copy-start(s32[8,8]{1,0:T(8,128)} %param.12) | copy-start | bytes 772
  16.9 7.6 %copy-start.2 = (bf16[8,7168]{1,0:T(8,128)(2,1)S(1)}, bf16[8,7168]{1,0:T(8,128)(2,1)}, u32[]{:S(2)}) copy-start(bf16[8,7168]{1,0:T(8,128)(2,1)} %param.10) | copy-start | bytes 344068
  16.9 91.0 %all-to-all-start = ((bf16[32,5,7168]{2,1,0:T(8,128)(2,1)}), bf16[32,5,7168]{2,1,0:T(8,128)(2,1)}, u32[]{:S(2)}, u32[]{:S(2)}) async-start(bf16[32,5,7168]{2,1,0:T(8,128)(2,1)} %bitcast.66), calls=%async_computation | async-start | bytes 7340032 | tf_op jit(solution)/shard_map/all_to_all | solution.py:57
  110.4 87.2 %all-to-all-start.2 = ((bf16[32,5,7168]{2,1,0:T(8,128)(2,1)}), bf16[32,5,7168]{2,1,0:T(8,128)(2,1)}, u32[]{:S(2)}, u32[]{:S(2)}) async-start(bf16[32,5,7168]{2,1,0:T(8,128)(2,1)} %bitcast.67), calls=%async_computation.3 | async-start | bytes 7340032 | tf_op jit(solution)/shard_map/all_to_all | solution.py:58
  113.9 135.9 %reduce-scatter.5.cloned.1.call-start = ((), (), s32[]{:S(2)}) async-start(), calls=%async_computation.6 | async-start | bytes 3440640 | tf_op jit(solution)/shard_map/reduce_scatter | solution.py:72
  202.1 12.4 %slice-start = ((s8[7340032]{0:T(1024)(128)(4,1)}), s8[4194304]{0:T(1024)(128)(4,1)S(1)}, s32[]{:S(2)}) async-start(s8[7340032]{0:T(1024)(128)(4,1)} %bitcast.64), calls=%async_computation.7 | async-start | bytes 8388608
  208.7 5.8 %slice-start.1 = ((s8[7340032]{0:T(1024)(128)(4,1)}), s8[3145728]{0:T(1024)(128)(4,1)S(1)}, s32[]{:S(2)}) async-start(s8[7340032]{0:T(1024)(128)(4,1)} %bitcast.64), calls=%async_computation.8 | async-start | bytes 6291456
  218.5 67.6 %reduce-scatter.3.cloned.1.call-start = ((), (), s32[]{:S(2)}) async-start(), calls=%async_computation.5 | async-start | bytes 3440640 | tf_op jit(solution)/shard_map/reduce_scatter | solution.py:66
  253.3 6.9 %collective-permute-start = (bf16[1,1,5,7168]{3,2,0,1:T(8,128)(2,1)S(1)}, bf16[1,1,5,7168]{3,2,0,1:T(8,128)(2,1)S(1)}, u32[]{:S(2)}, u32[]{:S(2)}) collective-permute-start(bf16[1,1,5,7168]{3,2,0,1:T(8,128)(2,1)S(1)} %constant_dynamic-slice_fusion.14), channel_id=1, source_target_pairs={{0,1},{1,2},{2,3},{3,4},{4,5},{5,6},{6,7},{7,8},{8,9},{9,10},{10,1... | collective-permute-start | bytes 215048 | tf_op jit(solution)/shard_map/ppermute | solution.py:30
  262.6 37.5 %collective-permute-start.1 = (bf16[1,1,5,7168]{3,2,0,1:T(8,128)(2,1)}, bf16[1,1,5,7168]{3,2,0,1:T(8,128)(2,1)S(1)}, u32[]{:S(2)}, u32[]{:S(2)}) collective-permute-start(bf16[1,1,5,7168]{3,2,0,1:T(8,128)(2,1)} %get-tuple-element.23), channel_id=1, source_target_pairs={{0,2},{1,3},{2,4},{3,5},{4,6},{5,7},{6,8},{7,9},{8,10},{9,11},{10,... | collective-permute-start | bytes 215048 | tf_op jit(solution)/shard_map/ppermute | solution.py:30
  288.7 11.4 %copy-start.8 = (bf16[1,1,5,7168]{3,2,0,1:T(8,128)(2,1)S(1)}, bf16[1,1,5,7168]{3,2,0,1:T(8,128)(2,1)}, u32[]{:S(2)}) copy-start(bf16[1,1,5,7168]{3,2,0,1:T(8,128)(2,1)} %get-tuple-element.22) | copy-start | bytes 215044
  288.7 49.6 %copy-start.7 = (bf16[1,1,5,7168]{3,2,0,1:T(8,128)(2,1)S(1)}, bf16[1,1,5,7168]{3,2,0,1:T(8,128)(2,1)}, u32[]{:S(2)}) copy-start(bf16[1,1,5,7168]{3,2,0,1:T(8,128)(2,1)} %get-tuple-element.21) | copy-start | bytes 215044
  288.7 56.3 %copy-start.6 = (bf16[1,1,5,7168]{3,2,0,1:T(8,128)(2,1)S(1)}, bf16[1,1,5,7168]{3,2,0,1:T(8,128)(2,1)}, u32[]{:S(2)}) copy-start(bf16[1,1,5,7168]{3,2,0,1:T(8,128)(2,1)} %get-tuple-element.20) | copy-start | bytes 215044
  288.7 63.8 %copy-start.5 = (bf16[1,1,5,7168]{3,2,0,1:T(8,128)(2,1)S(1)}, bf16[1,1,5,7168]{3,2,0,1:T(8,128)(2,1)}, u32[]{:S(2)}) copy-start(bf16[1,1,5,7168]{3,2,0,1:T(8,128)(2,1)} %get-tuple-element.19) | copy-start | bytes 215044
  288.7 71.9 %copy-start.4 = (bf16[1,1,5,7168]{3,2,0,1:T(8,128)(2,1)S(1)}, bf16[1,1,5,7168]{3,2,0,1:T(8,128)(2,1)}, u32[]{:S(2)}) copy-start(bf16[1,1,5,7168]{3,2,0,1:T(8,128)(2,1)} %get-tuple-element.18) | copy-start | bytes 215044
  288.7 77.0 %copy-start.3 = (bf16[1,1,5,7168]{3,2,0,1:T(8,128)(2,1)S(1)}, bf16[1,1,5,7168]{3,2,0,1:T(8,128)(2,1)}, u32[]{:S(2)}) copy-start(bf16[1,1,5,7168]{3,2,0,1:T(8,128)(2,1)} %get-tuple-element.17) | copy-start | bytes 215044
  288.8 157.2 %all-to-all-start.1 = ((bf16[16,5,7168]{2,1,0:T(8,128)(2,1)}), bf16[16,5,7168]{2,1,0:T(8,128)(2,1)}, u32[]{:S(2)}, u32[]{:S(2)}) async-start(bf16[16,5,7168]{2,1,0:T(8,128)(2,1)} %reshape.127), calls=%async_computation.2 | async-start | bytes 3670016 | tf_op jit(solution)/shard_map/all_to_all | solution.py:80
  294.6 102.6 %collective-permute-start.14 = (bf16[1,1,5,7168]{3,2,0,1:T(8,128)(2,1)S(1)}, bf16[1,1,5,7168]{3,2,0,1:T(8,128)(2,1)S(1)}, u32[]{:S(2)}, u32[]{:S(2)}) collective-permute-start(bf16[1,1,5,7168]{3,2,0,1:T(8,128)(2,1)S(1)} %get-tuple-element.10), channel_id=1, source_target_pairs={{0,15},{1,0},{2,1},{3,2},{4,3},{5,4},{6,5},{7,6},{8,7},{9,8},{10,9... | collective-permute-start | bytes 215048 | tf_op jit(solution)/shard_map/ppermute | solution.py:30
  298.9 97.6 %collective-permute-start.13 = (bf16[1,1,5,7168]{3,2,0,1:T(8,128)(2,1)S(1)}, bf16[1,1,5,7168]{3,2,0,1:T(8,128)(2,1)S(1)}, u32[]{:S(2)}, u32[]{:S(2)}) collective-permute-start(bf16[1,1,5,7168]{3,2,0,1:T(8,128)(2,1)S(1)} %get-tuple-element.11), channel_id=1, source_target_pairs={{0,14},{1,15},{2,0},{3,1},{4,2},{5,3},{6,4},{7,5},{8,6},{9,7},{10,... | collective-permute-start | bytes 215048 | tf_op jit(solution)/shard_map/ppermute | solution.py:30
  299.4 96.4 %collective-permute-start.12 = (bf16[1,1,5,7168]{3,2,0,1:T(8,128)(2,1)S(1)}, bf16[1,1,5,7168]{3,2,0,1:T(8,128)(2,1)S(1)}, u32[]{:S(2)}, u32[]{:S(2)}) collective-permute-start(bf16[1,1,5,7168]{3,2,0,1:T(8,128)(2,1)S(1)} %get-tuple-element.12), channel_id=1, source_target_pairs={{0,13},{1,14},{2,15},{3,0},{4,1},{5,2},{6,3},{7,4},{8,5},{9,6},{10... | collective-permute-start | bytes 215048 | tf_op jit(solution)/shard_map/ppermute | solution.py:30
  299.5 95.6 %collective-permute-start.11 = (bf16[1,1,5,7168]{3,2,0,1:T(8,128)(2,1)S(1)}, bf16[1,1,5,7168]{3,2,0,1:T(8,128)(2,1)S(1)}, u32[]{:S(2)}, u32[]{:S(2)}) collective-permute-start(bf16[1,1,5,7168]{3,2,0,1:T(8,128)(2,1)S(1)} %get-tuple-element.13), channel_id=1, source_target_pairs={{0,12},{1,13},{2,14},{3,15},{4,0},{5,1},{6,2},{7,3},{8,4},{9,5},{1... | collective-permute-start | bytes 215048 | tf_op jit(solution)/shard_map/ppermute | solution.py:30
  300.1 38.2 %collective-permute-start.2 = (bf16[1,1,5,7168]{3,2,0,1:T(8,128)(2,1)S(1)}, bf16[1,1,5,7168]{3,2,0,1:T(8,128)(2,1)S(1)}, u32[]{:S(2)}, u32[]{:S(2)}) collective-permute-start(bf16[1,1,5,7168]{3,2,0,1:T(8,128)(2,1)S(1)} %copy-done.8), channel_id=1, source_target_pairs={{0,3},{1,4},{2,5},{3,6},{4,7},{5,8},{6,9},{7,10},{8,11},{9,12},{10... | collective-permute-start | bytes 215048 | tf_op jit(solution)/shard_map/ppermute | solution.py:30
  338.3 6.7 %collective-permute-start.3 = (bf16[1,1,5,7168]{3,2,0,1:T(8,128)(2,1)S(1)}, bf16[1,1,5,7168]{3,2,0,1:T(8,128)(2,1)S(1)}, u32[]{:S(2)}, u32[]{:S(2)}) collective-permute-start(bf16[1,1,5,7168]{3,2,0,1:T(8,128)(2,1)S(1)} %copy-done.7), channel_id=1, source_target_pairs={{0,4},{1,5},{2,6},{3,7},{4,8},{5,9},{6,10},{7,11},{8,12},{9,13},{1... | collective-permute-start | bytes 215048 | tf_op jit(solution)/shard_map/ppermute | solution.py:30
  345.0 7.5 %collective-permute-start.4 = (bf16[1,1,5,7168]{3,2,0,1:T(8,128)(2,1)S(1)}, bf16[1,1,5,7168]{3,2,0,1:T(8,128)(2,1)S(1)}, u32[]{:S(2)}, u32[]{:S(2)}) collective-permute-start(bf16[1,1,5,7168]{3,2,0,1:T(8,128)(2,1)S(1)} %copy-done.6), channel_id=1, source_target_pairs={{0,5},{1,6},{2,7},{3,8},{4,9},{5,10},{6,11},{7,12},{8,13},{9,14},{... | collective-permute-start | bytes 215048 | tf_op jit(solution)/shard_map/ppermute | solution.py:30
  352.5 8.2 %collective-permute-start.5 = (bf16[1,1,5,7168]{3,2,0,1:T(8,128)(2,1)S(1)}, bf16[1,1,5,7168]{3,2,0,1:T(8,128)(2,1)S(1)}, u32[]{:S(2)}, u32[]{:S(2)}) collective-permute-start(bf16[1,1,5,7168]{3,2,0,1:T(8,128)(2,1)S(1)} %copy-done.5), channel_id=1, source_target_pairs={{0,6},{1,7},{2,8},{3,9},{4,10},{5,11},{6,12},{7,13},{8,14},{9,15},... | collective-permute-start | bytes 215048 | tf_op jit(solution)/shard_map/ppermute | solution.py:30
  360.7 5.1 %collective-permute-start.6 = (bf16[1,1,5,7168]{3,2,0,1:T(8,128)(2,1)S(1)}, bf16[1,1,5,7168]{3,2,0,1:T(8,128)(2,1)S(1)}, u32[]{:S(2)}, u32[]{:S(2)}) collective-permute-start(bf16[1,1,5,7168]{3,2,0,1:T(8,128)(2,1)S(1)} %copy-done.4), channel_id=1, source_target_pairs={{0,7},{1,8},{2,9},{3,10},{4,11},{5,12},{6,13},{7,14},{8,15},{9,0},... | collective-permute-start | bytes 215048 | tf_op jit(solution)/shard_map/ppermute | solution.py:30
  365.8 11.4 %collective-permute-start.7 = (bf16[1,1,5,7168]{3,2,0,1:T(8,128)(2,1)S(1)}, bf16[1,1,5,7168]{3,2,0,1:T(8,128)(2,1)S(1)}, u32[]{:S(2)}, u32[]{:S(2)}) collective-permute-start(bf16[1,1,5,7168]{3,2,0,1:T(8,128)(2,1)S(1)} %copy-done.3), channel_id=1, source_target_pairs={{0,8},{1,9},{2,10},{3,11},{4,12},{5,13},{6,14},{7,15},{8,0},{9,1},... | collective-permute-start | bytes 215048 | tf_op jit(solution)/shard_map/ppermute | solution.py:30
  377.1 5.1 %collective-permute-start.8 = (bf16[1,1,5,7168]{3,2,0,1:T(8,128)(2,1)S(1)}, bf16[1,1,5,7168]{3,2,0,1:T(8,128)(2,1)S(1)}, u32[]{:S(2)}, u32[]{:S(2)}) collective-permute-start(bf16[1,1,5,7168]{3,2,0,1:T(8,128)(2,1)S(1)} %get-tuple-element.16), channel_id=1, source_target_pairs={{0,9},{1,10},{2,11},{3,12},{4,13},{5,14},{6,15},{7,0},{8,1},{9,2},... | collective-permute-start | bytes 215048 | tf_op jit(solution)/shard_map/ppermute | solution.py:30
  382.3 6.1 %collective-permute-start.9 = (bf16[1,1,5,7168]{3,2,0,1:T(8,128)(2,1)S(1)}, bf16[1,1,5,7168]{3,2,0,1:T(8,128)(2,1)S(1)}, u32[]{:S(2)}, u32[]{:S(2)}) collective-permute-start(bf16[1,1,5,7168]{3,2,0,1:T(8,128)(2,1)S(1)} %get-tuple-element.15), channel_id=1, source_target_pairs={{0,10},{1,11},{2,12},{3,13},{4,14},{5,15},{6,0},{7,1},{8,2},{9,3},... | collective-permute-start | bytes 215048 | tf_op jit(solution)/shard_map/ppermute | solution.py:30
  388.4 6.1 %collective-permute-start.10 = (bf16[1,1,5,7168]{3,2,0,1:T(8,128)(2,1)S(1)}, bf16[1,1,5,7168]{3,2,0,1:T(8,128)(2,1)S(1)}, u32[]{:S(2)}, u32[]{:S(2)}) collective-permute-start(bf16[1,1,5,7168]{3,2,0,1:T(8,128)(2,1)S(1)} %get-tuple-element.14), channel_id=1, source_target_pairs={{0,11},{1,12},{2,13},{3,14},{4,15},{5,0},{6,1},{7,2},{8,3},{9,4},{... | collective-permute-start | bytes 215048 | tf_op jit(solution)/shard_map/ppermute | solution.py:30
  399.5 1.8 copy-start
  399.5 1.8 copy-start.1
Sparse Core Ops, SparseCore 0:
  218.7 31.0 reduce-scatter.4
  252.0 34.0 reduce-scatter.2
